TPU v7x, 32 devices: a whole 2x2x4 slice. The times are simulated.
32 devices in a mesh: dp: 16 (over z, y, core), rep: 2 (over x).
Axes of the slice: x: 2, y: 2, z: 4, core: 2. Of those that a mesh axis runs over, the one named last changes fastest.
Arguments:
- inputs: bfloat16 [32, 256, 768], P(('dp', 'rep')), may hold values from -6 to 6
- norm_gain: float32 [768], replicated, may hold values from 0.5 to 1.5
- in_weight: bfloat16 [768, 3352], P('dp'), may hold values from -0.21875 to 0.21875
- conv_weight: float32 [4, 1792], replicated, may hold values from -3 to 3
- conv_bias: float32 [1792], replicated, may hold values from -3 to 3
- dt_bias: float32 [24], replicated, may hold values from -6 to -1
- a_log: float32 [24], replicated, may hold values from -2 to 1.5
- skip_gain: float32 [24], replicated, may hold values from 0.5 to 2
- gate_gain: float32 [1536], replicated, may hold values from 0.5 to 1.5
- out_weight: bfloat16 [1536, 768], P('dp'), may hold values from -0.15625 to 0.15625
- cotangent: bfloat16 [32, 256, 768], P(('dp', 'rep')), may hold values from -6 to 6
Outputs:
- output: bfloat16 [32, 256, 768], P(('dp', 'rep'))
- grad_inputs: bfloat16 [32, 256, 768], P(('dp', 'rep'))
- grad_norm_gain: float32 [768], replicated
- grad_in_weight: float32 [768, 3352], P('dp')
- grad_conv_weight: float32 [4, 1792], replicated
- grad_conv_bias: float32 [1792], replicated
- grad_dt_bias: float32 [24], replicated
- grad_a_log: float32 [24], replicated
- grad_skip_gain: float32 [24], replicated
- grad_gate_gain: float32 [1536], replicated
- grad_out_weight: float32 [1536, 768], P('dp')
All inputs are finite; a program needn't handle non-finite values.
Results may differ from a plain program's by a relative error of at most 0.0082.
Values may be sent and summed in bfloat16 or wider, within the bound.
A program may use at most 128 MiB of HBM per device.

v0:
```python
import jax
import jax.numpy as jnp
from jax import lax
from jax.sharding import PartitionSpec as P

SPAN = 256


def head_mix(values, step_size, decay_rate, b_blocks, c_blocks, scores):
    length = values.shape[1]
    scaled = step_size * decay_rate
    running = jnp.cumsum(scaled, axis=1)
    row_ids = lax.broadcasted_iota(jnp.int32, (length, length), 0)
    col_ids = lax.broadcasted_iota(jnp.int32, (length, length), 1)
    causal = row_ids >= col_ids
    spread = running[:, :, None] - running[:, None, :]
    decays = jnp.exp(jnp.where(causal[None], spread, -jnp.inf))
    weight = scores * decays * step_size[:, None, :]
    within = jnp.einsum("cqs,csp->cqp", weight, values, precision=lax.Precision.HIGHEST)
    to_end = jnp.exp(running[:, -1:] - running) * step_size
    states = jnp.einsum(
        "cs,csn,csp->cnp", to_end, b_blocks, values, precision=lax.Precision.HIGHEST
    )
    before = jnp.zeros(states.shape[1:], states.dtype)
    priors = [before]
    carried = jnp.stack(priors)
    across = jnp.einsum("cqn,cnp->cqp", c_blocks, carried, precision=lax.Precision.HIGHEST)
    return within + across * jnp.exp(running)[:, :, None]


def mixer(projected, conv_weight, conv_bias, dt_bias, a_log, skip_gain, gate_gain):
    length = projected.shape[0]
    inner_width = gate_gain.shape[0]
    head_count = skip_gain.shape[0]
    channels = conv_bias.shape[0]
    state_width = (channels - inner_width) // 2
    tap_count = conv_weight.shape[0]
    gate_in = projected[:, :inner_width]
    conv_in = projected[:, inner_width : inner_width + channels]
    step_raw = projected[:, inner_width + channels :]
    padded = jnp.pad(conv_in, ((tap_count - 1, 0), (0, 0)))
    convolved = conv_bias + jnp.zeros_like(conv_in)
    for offset in range(tap_count):
        convolved = convolved + conv_weight[offset] * padded[offset : offset + length]
    active = jax.nn.silu(convolved)
    values = active[:, :inner_width]
    b_proj = active[:, inner_width : inner_width + state_width]
    c_proj = active[:, inner_width + state_width :]
    step_size = jax.nn.softplus(step_raw + dt_bias)
    decay_rate = -jnp.exp(a_log)
    blocks = length // SPAN
    b_blocks = b_proj.reshape(blocks, SPAN, state_width)
    c_blocks = c_proj.reshape(blocks, SPAN, state_width)
    scores = jnp.einsum("cqn,csn->cqs", c_blocks, b_blocks, precision=lax.Precision.HIGHEST)
    head_values = values.reshape(blocks, SPAN, head_count, inner_width // head_count).transpose(
        2, 0, 1, 3
    )
    head_steps = step_size.reshape(blocks, SPAN, head_count).transpose(2, 0, 1)

    def one_head(member):
        return head_mix(member[0], member[1], member[2], b_blocks, c_blocks, scores)

    mixed_heads = lax.map(jax.checkpoint(one_head), (head_values, head_steps, decay_rate))
    scanned = mixed_heads.transpose(1, 2, 0, 3).reshape(length, inner_width)
    skipped = values.reshape(length, head_count, inner_width // head_count) * skip_gain[:, None]
    scanned = scanned + skipped.reshape(length, inner_width)
    gated_out = scanned * jax.nn.silu(gate_in)
    return (
        gated_out
        * lax.rsqrt(jnp.mean(gated_out * gated_out, axis=-1, keepdims=True) + 1e-05)
        * gate_gain
    )


def front_norm(rows_in, norm_gain):
    return (
        rows_in * lax.rsqrt(jnp.mean(rows_in * rows_in, axis=-1, keepdims=True) + 1e-05) * norm_gain
    )


def local(
    inputs,
    norm_gain,
    in_weight,
    conv_weight,
    conv_bias,
    dt_bias,
    a_log,
    skip_gain,
    gate_gain,
    out_weight,
    cotangent,
):
    in_full, out_full = (
        lax.all_gather(in_weight, "dp", axis=0, tiled=True),
        lax.all_gather(out_weight, "dp", axis=0, tiled=True),
    )
    seq_count, length, model_width = inputs.shape
    total_rows = seq_count * length
    rows_in = inputs.astype(jnp.float32).reshape(total_rows, model_width)
    normed, norm_back = jax.vjp(front_norm, rows_in, norm_gain)
    normed_low = normed.astype(jnp.bfloat16)
    projected = jnp.dot(normed_low, in_full, preferred_element_type=jnp.float32)
    projected = projected.reshape(seq_count, length, projected.shape[-1])
    mix_all = jax.vmap(mixer, in_axes=(0, None, None, None, None, None, None))
    mixed, mix_back = jax.vjp(
        mix_all, projected, conv_weight, conv_bias, dt_bias, a_log, skip_gain, gate_gain
    )
    mixed_low = mixed.reshape(total_rows, mixed.shape[-1]).astype(jnp.bfloat16)
    result = rows_in + jnp.dot(mixed_low, out_full, preferred_element_type=jnp.float32)
    output = result.astype(jnp.bfloat16).reshape(inputs.shape)
    in_back, out_back = (
        lax.all_gather(in_weight, "dp", axis=0, tiled=True),
        lax.all_gather(out_weight, "dp", axis=0, tiled=True),
    )
    cotangent_rows = cotangent.reshape(total_rows, model_width)
    grad_out_w = jnp.einsum(
        "rk,rd->kd", mixed_low, cotangent_rows, preferred_element_type=jnp.float32
    )
    grad_mixed = jnp.einsum(
        "rd,kd->rk", cotangent_rows, out_back, preferred_element_type=jnp.float32
    )
    mix_grads = mix_back(grad_mixed.reshape(mixed.shape))
    grad_proj_low = mix_grads[0].reshape(total_rows, projected.shape[-1]).astype(jnp.bfloat16)
    grad_in_w = jnp.einsum(
        "rd,rp->dp", normed_low, grad_proj_low, preferred_element_type=jnp.float32
    )
    grad_normed = jnp.einsum(
        "rp,dp->rd", grad_proj_low, in_back, preferred_element_type=jnp.float32
    )
    grad_rows, grad_norm = norm_back(grad_normed)
    grad_inputs = (
        (cotangent_rows.astype(jnp.float32) + grad_rows).astype(jnp.bfloat16).reshape(inputs.shape)
    )
    half_in, half_out = (
        lax.psum_scatter(grad_in_w, ("dp", "rep"), scatter_dimension=0, tiled=True),
        lax.psum_scatter(grad_out_w, ("dp", "rep"), scatter_dimension=0, tiled=True),
    )
    owned_in, owned_out = (
        lax.all_gather(half_in.astype(jnp.bfloat16), "rep", axis=0, tiled=True).astype(
            half_in.dtype
        ),
        lax.all_gather(half_out.astype(jnp.bfloat16), "rep", axis=0, tiled=True).astype(
            half_out.dtype
        ),
    )
    summed = lax.psum(
        (
            grad_norm,
            mix_grads[1],
            mix_grads[2],
            mix_grads[3],
            mix_grads[4],
            mix_grads[5],
            mix_grads[6],
        ),
        ("dp", "rep"),
    )
    return (
        output,
        grad_inputs,
        summed[0],
        owned_in,
        summed[1],
        summed[2],
        summed[3],
        summed[4],
        summed[5],
        summed[6],
        owned_out,
    )


def solution(mesh):
    placed = (
        P(("dp", "rep"), None, None),
        P(),
        P("dp", None),
        P(),
        P(),
        P(),
        P(),
        P(),
        P(),
        P("dp", None),
        P(("dp", "rep"), None, None),
    )
    return jax.shard_map(
        local,
        mesh=mesh,
        in_specs=placed,
        out_specs=(
            P(("dp", "rep"), None, None),
            P(("dp", "rep"), None, None),
            P(),
            P("dp", None),
            P(),
            P(),
            P(),
            P(),
            P(),
            P(),
            P("dp", None),
        ),
        check_vma=False,
    )
```

profile of v0, /device:TPU:0, one launch (start us, length us, event | category | flops | bytes accessed | tf_op | source)
XLA Modules:
  0.0 713.6 jit_solution(2319859396425935077)
XLA Ops:
  12.4 56.8 %all-gather.3.cloned.1.call-done = bf16[768,3352]{1,0:T(8,128)(2,1)} async-done(((bf16[48,3352]{1,0:T(8,128)(2,1)}), bf16[768,3352]{1,0:T(8,128)(2,1)}) %all-gather.3.cloned.1.call-update) | async-done | bytes 5148688 | tf_op jit(solution)/shard_map/all_gather | solution.py:95
  69.2 5.0 convolution_bitcast_fusion.3
  74.9 4.0 fusion.50
  80.5 2.3 copy.55
  83.0 83.4 %while.35 = (s32[]{:T(128)}, f32[24,1,1,256,64]{3,4,2,1,0:T(8,128)S(1)}, f32[24,1,1,256]{3,2,1,0:T(1,128)S(1)}, f32[24]{0:T(128)S(1)}, f32[1,1,256,256]{3,2,1,0:...) while((s32[]{:T(128)}, ...), condition=%wide.region_4.5_spmd.clone, body=%wide.region_1.4_spmd.clone.sunk | while | flops 50725124 | bytes 539837 | solution.py:63
  167.6 2.5 multiply_reduce_fusion.6
  171.2 3.0 fusion.82
  174.2 4.3 fusion.54
  180.5 4.9 multiply_reduce_fusion.5
  186.7 347.8 %while.36 = (s32[]{:T(128)}, f32[1,1,256,256]{3,2,1,0:T(8,128)}, f32[1,1,256,128]{3,2,1,0:T(8,128)}, f32[24,1,1,256,64]{3,4,2,1,0:T(8,128)}, f32[24,1,1,256]{3,0...) while((s32[]{:T(128)}, f32[1,1,256,256]{3,2,1,0:T(8,128)}, ...), condition=%wide.region_17.18_spmd.clone, body=%wide.region_7.17_spmd.clone.sunk | while | flops 152684288 | bytes 3709364 | solution.py:63
  191.9 2.3 fusion.149
  205.4 2.4 fusion.149
  207.8 2.0 fusion.150
  220.0 2.4 fusion.149
  222.3 2.0 fusion.150
  234.5 2.3 fusion.149
  249.1 2.3 fusion.149
  251.4 2.0 fusion.150
  263.6 2.4 fusion.149
  265.9 2.0 fusion.150
  278.1 2.4 fusion.149
  280.5 2.0 fusion.150
  292.6 2.3 fusion.149
  307.2 2.3 fusion.149
  321.7 2.3 fusion.149
  336.2 2.3 fusion.149
  350.8 2.3 fusion.149
  365.3 2.3 fusion.149
  379.8 2.3 fusion.149
  394.3 2.3 fusion.149
  408.9 2.3 fusion.149
  423.4 2.3 fusion.149
  437.9 2.3 fusion.149
  452.4 2.3 fusion.149
  467.0 2.3 fusion.149
  481.5 2.3 fusion.149
  496.0 2.3 fusion.149
  510.5 2.3 fusion.149
  525.1 2.3 fusion.149
  540.4 2.3 multiply_add_fusion.1
  543.3 4.6 multiply_reduce_fusion.3
  552.3 5.8 fusion.79
  559.1 5.5 fusion.68
  564.7 40.6 %all-reduce.16 = (f32[768]{0:T(1024)}, f32[4,1792]{1,0:T(4,128)}, f32[1792]{0:T(1024)}, f32[24]{0:T(128)}, f32[24]{0:T(128)}, /*index=5*/f32[24]{0:T(128)}, f32[1536]{0:T(1024)}) all-reduce(f32[768]{0:T(1024)S(1)} %get-tuple-element.481, f32[4,1792]{1,0:T(4,128)S(1)} %pad_add_fusion.3, ...), channel_id=1, replica_groups=mesh['dp'=16,'rep'=2] {'dp','rep'}, use_global_device_ids=true, to_apply=%region_20.21 | all-reduce | flops 11336 | bytes 90688 | tf_op jit(solution)/shard_map/psum | solution.py:147
  606.3 3.4 fusion.58
  610.7 6.9 all_gather.17
  618.3 80.9 %reduce-scatter.7.cloned.1.call-done = f32[24,3352]{1,0:T(8,128)} async-done(((f32[768,3352]{1,0:T(8,128)}), f32[24,3352]{1,0:T(8,128)}) %reduce-scatter.7.cloned.1.call-update) | async-done | bytes 321808
  700.2 6.0 all_gather.16
  (1017 shorter events, 393.0 us)
Async XLA Ops:
  7.2 62.1 %all-gather.3.cloned.1.call-start = ((), (), s32[]{:S(2)}) async-start(), calls=%async_computation.2 | async-start | bytes 5640192 | tf_op jit(solution)/shard_map/all_gather | solution.py:95
  7.9 166.3 %all-gather.5.cloned.1.call-start = ((), (), s32[]{:S(2)}) async-start(), calls=%async_computation.3 | async-start | bytes 2506752 | tf_op jit(solution)/shard_map/all_gather | solution.py:96
  8.7 601.1 %reduce-scatter.5.cloned.1.call-start = ((), (), s32[]{:S(2)}) async-start(), calls=%async_computation.4 | async-start | bytes 4866048 | tf_op jit(solution)/shard_map/reduce_scatter | solution.py:137
  9.9 64.3 %copy-start.29 = (f32[256]{0:T(256)}, f32[256]{0:T(256)S(1)}, u32[]{:S(2)}) copy-start(f32[256]{0:T(256)S(1)} %fusion.104) | copy-start | bytes 3076
  11.6 62.8 %copy-start.15 = (f32[1792]{0:T(1024)}, f32[1792]{0:T(1024)S(1)}, u32[]{:S(2)}) copy-start(f32[1792]{0:T(1024)S(1)} %get-tuple-element.483) | copy-start | bytes 21508
  11.6 62.8 %copy-start.17 = (f32[1792]{0:T(1024)}, f32[1792]{0:T(1024)S(1)}, u32[]{:S(2)}) copy-start(f32[1792]{0:T(1024)S(1)} %get-tuple-element.484) | copy-start | bytes 21508
  11.6 62.8 %copy-start.19 = (f32[1792]{0:T(1024)}, f32[1792]{0:T(1024)S(1)}, u32[]{:S(2)}) copy-start(f32[1792]{0:T(1024)S(1)} %get-tuple-element.485) | copy-start | bytes 21508
  11.6 62.8 %copy-start.21 = (f32[1792]{0:T(1024)}, f32[1792]{0:T(1024)S(1)}, u32[]{:S(2)}) copy-start(f32[1792]{0:T(1024)S(1)} %get-tuple-element.486) | copy-start | bytes 21508
  74.2 6.2 copy-start
  74.4 4.6 copy-start.2
  179.9 519.4 %reduce-scatter.7.cloned.1.call-start = ((), (), s32[]{:S(2)}) async-start(), calls=%async_computation.5 | async-start | bytes 10948608
  180.5 6.2 copy-start.40
  191.8 4.3 copy-start.8
  205.4 4.3 copy-start.11
  205.4 5.3 copy-start.8
  220.0 5.3 copy-start.8
  234.5 5.3 copy-start.8
  249.0 5.3 copy-start.8
  263.6 4.3 copy-start.11
  263.6 5.3 copy-start.8
  278.1 4.3 copy-start.11
  278.1 5.3 copy-start.8
  292.6 5.3 copy-start.8
  307.2 5.3 copy-start.8
  321.7 5.3 copy-start.8
  336.2 5.3 copy-start.8
  350.8 5.3 copy-start.8
  365.3 5.3 copy-start.8
  379.8 5.3 copy-start.8
  394.3 5.3 copy-start.8
  408.9 5.3 copy-start.8
  423.4 5.3 copy-start.8
  437.9 5.3 copy-start.8
  452.4 5.3 copy-start.8
  466.9 5.3 copy-start.8
  481.5 5.3 copy-start.8
  496.0 5.3 copy-start.8
  510.5 5.3 copy-start.8
  525.0 5.3 copy-start.8
  537.9 4.8 copy-start.3
  543.3 4.6 copy-start.16
  543.3 4.6 copy-start.18
  543.3 4.6 copy-start.20
  543.3 4.6 copy-start.22
  559.1 5.6 copy-start.27
  559.1 46.1 %copy-start.32 = (f32[256]{0:T(256)S(1)}, f32[256]{0:T(256)}, u32[]{:S(2)}) copy-start(f32[256]{0:T(256)} %copy-done.31) | copy-start | bytes 3076
  559.1 46.2 %copy-start.10 = (bf16[1,256,768]{2,1,0:T(8,128)(2,1)S(1)}, bf16[1,256,768]{2,1,0:T(8,128)(2,1)}, u32[]{:S(2)}) copy-start(bf16[1,256,768]{2,1,0:T(8,128)(2,1)} %param.25) | copy-start | bytes 1179652
  564.7 41.6 %copy-start.26 = (f32[256]{0:T(256)S(1)}, f32[256]{0:T(256)}, u32[]{:S(2)}) copy-start(f32[256]{0:T(256)} %copy-done.24) | copy-start | bytes 3076
  (45 other events, 132.9 us)
Sparse Core Ops, SparseCore 0:
  10.2 59.0 all-gather.2
  71.5 41.0 all-gather.4
  180.0 106.3 reduce-scatter.4
  558.3 140.8 reduce-scatter.6
where the time goes:
time: 719 us; the launch traced here: 714 us
  matrix products  198 us (28%)
  local copies, waits for them, and re-layouts  155 us (22%)
  other arithmetic  151 us (21%)
  waiting for transfers between devices  139 us (19%)
  blocking collectives  53.5 us (7%)
  between operations  14.3 us (2%)
    dot_general x72, matrix products, head_mix(): jnp.einsum('cqs,csp->cqp', weight, values, precision=lax.Precision.HIGHEST)  115 us
    unnamed x5, waiting for transfers between devices  82.3 us
    squeeze x72, local copies, waits for them, and re-layouts, mixer(): lax.map(jax.checkpoint(one_head), (head_values, head_steps, decay_rate))  74.2 us
    another operation x144, other arithmetic  58 us
    all_gather x1, waiting for transfers between devices, local(): lax.all_gather(in_weight, 'dp', axis=0, tiled=True)  56.8 us
    dot_general x49, matrix products, head_mix(): jnp.einsum('cqn,cnp->cqp', c_blocks, carried, precision=lax.Precision.HIG...  52.9 us
    psum x1, blocking collectives, local(): lax.psum((grad_norm, mix_grads[1], mix_grads[2], mix_grads[3], mix_grads[...  40.6 us
    mul x48, other arithmetic, head_mix(): scaled = step_size * decay_rate  31.2 us
  transfers between devices with their start and end apart: 4, of which 2 were waited for; matrix products, arithmetic and copies ran while one was open for 69% of the time, Pallas kernels for 0%

commit v1 on v0

--- a/solution.py
+++ b/solution.py
@@ -92,7 +92,9 @@
     cotangent,
 ):
     in_full, out_full = (
-        lax.all_gather(in_weight, "dp", axis=0, tiled=True),
+        jnp.concatenate(
+            lax.all_to_all(jnp.stack([in_weight] * lax.axis_size("dp")), "dp", 0, 0), axis=0
+        ),
         lax.all_gather(out_weight, "dp", axis=0, tiled=True),
     )
     seq_count, length, model_width = inputs.shape

time: 719 us -> 934 us (1.30)
  local copies, waits for them, and re-layouts: 155 us -> 222 us
  matrix products: 198 us -> 243 us
  waiting for transfers between devices: 139 us -> 179 us
  blocking collectives: 53.5 us -> 84.2 us
  other arithmetic: 151 us -> 174 us
    all_to_all x0 -> x1, waiting for transfers between devices: none -> 108 us  [local(): lax.all_to_all(jnp.stack([in_weight] * lax.axis_size('dp')), 'dp', 0, 0)]
    all_gather x1, waiting for transfers between devices: 56.8 us -> 0.01 us  [local(): lax.all_gather(in_weight, 'dp', axis=0, tiled=True)]
    psum x1, blocking collectives: 40.6 us -> 72.9 us  [local(): lax.psum((grad_norm, mix_grads[1], mix_grads[2], mix_grads[3], mix_grads[...]
    dynamic_slice x48, local copies, waits for them, and re-layouts: 28 us -> 59.6 us  [mixer(): lax.map(jax.checkpoint(one_head), (head_values, head_steps, decay_rate))]
    dynamic_update_slice x48, local copies, waits for them, and re-layouts: 19.2 us -> 46 us  [mixer(): lax.map(jax.checkpoint(one_head), (head_values, head_steps, decay_rate))]
    dot_general x72, matrix products: 115 us -> 137 us  [head_mix(): jnp.einsum('cqs,csp->cqp', weight, values, precision=lax.Precision.HIGHEST)]
    dot_general x49, matrix products: 52.9 us -> 74.6 us  [head_mix(): jnp.einsum('cqn,cnp->cqp', c_blocks, carried, precision=lax.Precision.HIG...]
    mul x48, other arithmetic: 31.2 us -> 47.4 us  [head_mix(): scaled = step_size * decay_rate]
  transfers between devices with their start and end apart: 4 -> 5, of which waited for: 2 -> 2; matrix products, arithmetic and copies ran while one was open for 69% -> 68% of each run, Pallas kernels for 0% -> 0%
where the time goes in v1:
time: 934 us; the launch traced here: 927 us
  matrix products  243 us (26%)
  local copies, waits for them, and re-layouts  222 us (24%)
  waiting for transfers between devices  179 us (19%)
  other arithmetic  174 us (19%)
  blocking collectives  84.2 us (9%)
  between operations  15.9 us (2%)
    dot_general x72, matrix products, head_mix(): jnp.einsum('cqs,csp->cqp', weight, values, precision=lax.Precision.HIGHEST)  137 us
    all_to_all x1, waiting for transfers between devices, local(): lax.all_to_all(jnp.stack([in_weight] * lax.axis_size('dp')), 'dp', 0, 0)  108 us
    dot_general x49, matrix products, head_mix(): jnp.einsum('cqn,cnp->cqp', c_blocks, carried, precision=lax.Precision.HIG...  74.6 us
    squeeze x72, local copies, waits for them, and re-layouts, mixer(): lax.map(jax.checkpoint(one_head), (head_values, head_steps, decay_rate))  74 us
    psum x1, blocking collectives, local(): lax.psum((grad_norm, mix_grads[1], mix_grads[2], mix_grads[3], mix_grads[...  72.9 us
    unnamed x5, waiting for transfers between devices  70.8 us
    dynamic_slice x48, local copies, waits for them, and re-layouts, mixer(): lax.map(jax.checkpoint(one_head), (head_values, head_steps, decay_rate))  59.6 us
    another operation x144, other arithmetic  58 us
  transfers between devices with their start and end apart: 5, of which 2 were waited for; matrix products, arithmetic and copies ran while one was open for 68% of the time, Pallas kernels for 0%

profile of v1, /device:TPU:0, one launch (start us, length us, event | category | flops | bytes accessed | tf_op | source)
XLA Modules:
  0.0 926.9 jit_solution(16370621282175115388)
XLA Ops:
  8.0 3.7 stack.2
  11.7 7.6 all-to-all-start
  22.5 108.0 %all-to-all-done = bf16[16,48,3352]{2,1,0:T(8,128)(2,1)} async-done(((bf16[16,48,3352]{2,1,0:T(8,128)(2,1)}), bf16[16,48,3352]{2,1,0:T(8,128)(2,1)}, u32[]{:S(2)}, u32[]{:S(2)}) %all-to-all-start) | async-done | bytes 5148704 | tf_op jit(solution)/shard_map/all_to_all | solution.py:96
  130.5 4.9 convolution_bitcast_fusion.3
  136.1 4.0 fusion.50
  142.8 3.3 copy.55
  147.0 115.3 %while.35 = (s32[]{:T(128)}, f32[24,1,1,256,64]{3,4,2,1,0:T(8,128)S(1)}, f32[24,1,1,256]{3,2,1,0:T(1,128)}, f32[24]{0:T(128)}, f32[1,1,256,256]{3,2,1,0:T(8,128)...) while((s32[]{:T(128)}, ...), condition=%wide.region_4.5_spmd.clone, body=%wide.region_1.4_spmd.clone.sunk | while | flops 50725124 | bytes 539829 | solution.py:63
  263.5 2.5 multiply_reduce_fusion.6
  266.1 4.4 fusion.54
  270.5 3.0 fusion.77
  273.5 4.9 multiply_reduce_fusion.5
  280.5 434.7 %while.36 = (s32[]{:T(128)}, f32[1,1,256,256]{3,2,1,0:T(8,128)}, f32[1,1,256,128]{3,2,1,0:T(8,128)}, f32[24,1,1,256,64]{3,4,2,1,0:T(8,128)}, f32[24,1,1,256]{3,0...) while((s32[]{:T(128)}, f32[1,1,256,256]{3,2,1,0:T(8,128)}, ...), condition=%wide.region_17.18_spmd.clone, body=%wide.region_7.17_spmd.clone.sunk | while | flops 152684288 | bytes 2136436 | solution.py:63
  286.3 2.2 fusion.143
  303.4 2.3 fusion.143
  313.9 2.0 fusion.144
  321.6 2.3 fusion.143
  332.1 2.0 fusion.144
  339.8 2.3 fusion.143
  358.0 2.3 fusion.143
  376.2 2.3 fusion.143
  394.3 2.3 fusion.143
  412.5 2.3 fusion.143
  430.6 2.3 fusion.143
  448.8 2.3 fusion.143
  466.9 2.3 fusion.143
  485.1 2.3 fusion.143
  503.2 2.3 fusion.143
  521.4 2.3 fusion.143
  539.5 2.3 fusion.143
  557.7 2.3 fusion.143
  575.8 2.3 fusion.143
  594.0 2.3 fusion.143
  612.1 2.3 fusion.143
  630.3 2.3 fusion.143
  648.4 2.3 fusion.143
  666.6 2.3 fusion.143
  684.7 2.3 fusion.143
  702.8 2.3 fusion.143
  721.1 2.3 multiply_add_fusion.1
  724.1 5.1 multiply_reduce_fusion.3
  733.4 5.7 fusion.87
  749.6 6.3 fusion.68
  756.0 72.9 %all-reduce.16 = (f32[768]{0:T(1024)}, f32[4,1792]{1,0:T(4,128)}, f32[1792]{0:T(1024)}, f32[24]{0:T(128)}, f32[24]{0:T(128)}, /*index=5*/f32[24]{0:T(128)}, f32[1536]{0:T(1024)}) all-reduce(f32[768]{0:T(1024)} %get-tuple-element.481, f32[4,1792]{1,0:T(4,128)} %pad_add_fusion.3, ...), channel_id=1, replica_groups=mesh['dp'=16,'rep'=2] {'dp','rep'}, use_global_device_ids=true, to_apply=%region_20.21 | all-reduce | flops 11336 | bytes 90688 | tf_op jit(solution)/shard_map/psum | solution.py:149
  829.6 2.3 fusion.75
  831.9 3.4 fusion.58
  836.2 5.3 all_gather.16
  842.2 69.4 %reduce-scatter.7.cloned.1.call-done = f32[24,3352]{1,0:T(8,128)} async-done(((f32[768,3352]{1,0:T(8,128)}), f32[24,3352]{1,0:T(8,128)}) %reduce-scatter.7.cloned.1.call-update) | async-done | bytes 321808
  912.6 6.0 all_gather.15
  (908 shorter events, 525.4 us)
Async XLA Ops:
  11.7 9.2 copy-start.31
  11.7 9.9 %copy-start.25 = (f32[4,1792]{1,0:T(4,128)S(1)}, f32[4,1792]{1,0:T(4,128)}, u32[]{:S(2)}) copy-start(f32[4,1792]{1,0:T(4,128)} %param.18) | copy-start | bytes 86020
  11.7 10.0 %copy-start.7 = (bf16[1,256,768]{2,1,0:T(8,128)(2,1)S(1)}, bf16[1,256,768]{2,1,0:T(8,128)(2,1)}, u32[]{:S(2)}) copy-start(bf16[1,256,768]{2,1,0:T(8,128)(2,1)} %param.15) | copy-start | bytes 1179652
  11.7 10.2 %copy-start.32 = (f32[24]{0:T(128)S(1)}, f32[24]{0:T(128)}, u32[]{:S(2)}) copy-start(f32[24]{0:T(128)} %param.21) | copy-start | bytes 292
  11.7 118.8 %copy-start.13 = (f32[768]{0:T(1024)S(1)}, f32[768]{0:T(1024)}, u32[]{:S(2)}) copy-start(f32[768]{0:T(1024)} %param.16) | copy-start | bytes 9220
  11.7 118.8 %all-to-all-start = ((bf16[16,48,3352]{2,1,0:T(8,128)(2,1)}), bf16[16,48,3352]{2,1,0:T(8,128)(2,1)}, u32[]{:S(2)}, u32[]{:S(2)}) async-start(bf16[16,48,3352]{2,1,0:T(8,128)(2,1)} %stack.2), calls=%async_computation | async-start | bytes 10616832 | tf_op jit(solution)/shard_map/all_to_all | solution.py:96
  19.3 246.7 %all-gather.3.cloned.1.call-start = ((), (), s32[]{:S(2)}) async-start(), calls=%async_computation.3 | async-start | bytes 2506752 | tf_op jit(solution)/shard_map/all_gather | solution.py:98
  20.1 729.6 %all-gather.5.cloned.1.call-start = ((), (), s32[]{:S(2)}) async-start(), calls=%async_computation.4 | async-start | bytes 5640192 | tf_op jit(solution)/shard_map/all_gather | solution.py:115
  20.8 814.5 %reduce-scatter.5.cloned.1.call-start = ((), (), s32[]{:S(2)}) async-start(), calls=%async_computation.5 | async-start | bytes 4866048 | tf_op jit(solution)/shard_map/reduce_scatter | solution.py:139
  21.7 113.8 %copy-start.17 = (f32[1792]{0:T(1024)}, f32[1792]{0:T(1024)S(1)}, u32[]{:S(2)}) copy-start(f32[1792]{0:T(1024)S(1)} %get-tuple-element.483) | copy-start | bytes 21508
  21.7 113.8 %copy-start.19 = (f32[1792]{0:T(1024)}, f32[1792]{0:T(1024)S(1)}, u32[]{:S(2)}) copy-start(f32[1792]{0:T(1024)S(1)} %get-tuple-element.484) | copy-start | bytes 21508
  21.7 113.8 %copy-start.21 = (f32[1792]{0:T(1024)}, f32[1792]{0:T(1024)S(1)}, u32[]{:S(2)}) copy-start(f32[1792]{0:T(1024)S(1)} %get-tuple-element.485) | copy-start | bytes 21508
  21.8 113.8 %copy-start.23 = (f32[1792]{0:T(1024)}, f32[1792]{0:T(1024)S(1)}, u32[]{:S(2)}) copy-start(f32[1792]{0:T(1024)S(1)} %get-tuple-element.486) | copy-start | bytes 21508
  21.9 113.4 %copy-start.28 = (f32[256]{0:T(256)}, f32[256]{0:T(256)S(1)}, u32[]{:S(2)}) copy-start(f32[256]{0:T(256)S(1)} %fusion.65) | copy-start | bytes 3076
  22.5 112.9 %copy-start.26 = (f32[256]{0:T(256)}, f32[256]{0:T(256)S(1)}, u32[]{:S(2)}) copy-start(f32[256]{0:T(256)S(1)} %fusion.98) | copy-start | bytes 3076
  135.4 10.8 %copy-start = (f32[1,256,3352]{1,2,0:T(8,128)}, f32[1,256,3352]{1,2,0:T(8,128)S(1)}, u32[]{:S(2)}) copy-start(f32[1,256,3352]{1,2,0:T(8,128)S(1)} %convolution_bitcast_fusion.3) | copy-start | bytes 10297348
  135.4 0.7 copy-start.29
  135.5 4.6 copy-start.4
  140.1 2.4 copy-start.2
  142.8 3.3 copy-start.30
  146.9 115.5 %copy-start.3 = (f32[1,256,1792]{1,2,0:T(8,128)S(1)}, f32[1,256,1792]{1,2,0:T(8,128)}, u32[]{:S(2)}) copy-start(f32[1,256,1792]{1,2,0:T(8,128)} %copy-done.2) | copy-start | bytes 5505028
  262.4 1.2 copy-start.6
  263.5 2.5 copy-start.12
  266.1 4.4 copy-start.11
  270.5 3.0 copy-start.14
  278.4 633.1 %reduce-scatter.7.cloned.1.call-start = ((), (), s32[]{:S(2)}) async-start(), calls=%async_computation.6 | async-start | bytes 10948608
  715.3 0.6 copy-start.15
  718.1 5.3 copy-start.5
  721.1 11.0 %copy-start.16 = (f32[1,256,24]{1,2,0:T(8,128)}, f32[1,256,24]{1,2,0:T(8,128)S(1)}, u32[]{:S(2)}) copy-start(f32[1,256,24]{1,2,0:T(8,128)S(1)} %get-tuple-element.541) | copy-start | bytes 73732
  721.1 2.9 copy-start.1
  724.1 5.1 copy-start.18
  724.1 5.1 copy-start.20
  724.1 5.2 copy-start.22
  724.1 5.2 copy-start.24
  730.5 2.9 copy-start.8
  730.5 2.9 copy-start.10
  730.5 2.9 copy-start.27
  732.2 1.3 copy-start.9
Sparse Core Ops, SparseCore 0:
  22.4 97.8 all-gather.2
  122.5 71.5 all-gather.4
Sparse Core Ops, SparseCore 1:
  278.5 137.5 reduce-scatter.4
  739.3 172.2 reduce-scatter.6
